TPU v7x, 128 devices: a whole 4x4x4 slice. The times are simulated.
128 devices in a mesh: seq: 32 (over x, y, core), head: 4 (over z).
Axes of the slice: x: 4, y: 4, z: 4, core: 2. Of those that a mesh axis runs over, the one named last changes fastest.
Arguments:
- queries: bfloat16 [2, 8192, 20, 128], P(None, ('seq', 'head')), may hold values from -96 to 96
- grad_out: bfloat16 [2, 8192, 20, 128], P(None, ('seq', 'head')), may hold values from -6 to 6
- keys: bfloat16 [8192, 4, 128], P('seq', 'head'), may hold values from -6 to 6
- values: bfloat16 [8192, 4, 128], P('seq', 'head'), may hold values from -6 to 6
- doc_start: int32 [8192], replicated, may hold values from 0 to 8191, as said below
Outputs:
- query_grads: bfloat16 [2, 8192, 20, 128], P(None, ('seq', 'head'))
- key_grads: bfloat16 [8192, 4, 128], P('seq', 'head')
- value_grads: bfloat16 [8192, 4, 128], P('seq', 'head')
Inputs may be any that keep to these rules, and one draw needn't show every extreme that they name: doc_start[i] is the first position of token i's document, so doc_start[i] <= i; it is 0 for every token before position 4096, at most four documents begin at or after it, and the last token begins a document of its own.
All inputs are finite; a program needn't handle non-finite values.
Results may differ from a plain program's by a relative error of at most 0.005.
Values may be sent and summed in bfloat16 or wider, within the bound.
A program may use at most 128 MiB of HBM per device.

v0:
```python
import math
import jax
import jax.numpy as jnp
from jax import lax
from jax.sharding import PartitionSpec as P

NEG_START = -1e30


def block_length(key_count):
    return math.gcd(key_count, 1024)


def over_blocks(advance, carried, pieces):
    key_count = pieces[0].shape[0]
    block_rows = block_length(key_count)

    def one_block(block_index, inner):
        block_start = block_index * block_rows
        sliced = tuple(
            (
                lax.dynamic_slice_in_dim(piece_rows, block_start, block_rows, 0)
                for piece_rows in pieces
            )
        )
        return advance(inner, sliced, block_start)

    return lax.fori_loop(0, key_count // block_rows, one_block, carried)


def masked_scores(group, key_block, key_start, score_scale):
    query_rows, grad_rows, starts, positions = group
    key_pos = key_start + jnp.arange(key_block.shape[0], dtype=jnp.int32)
    allowed = (key_pos[None, :] >= starts[:, None]) & (key_pos[None, :] <= positions[:, None])
    scores = (
        jnp.einsum("lrkgd,nkd->lkgrn", query_rows, key_block, preferred_element_type=jnp.float32)
        * score_scale
    )
    return jnp.where(allowed, scores, -jnp.inf)


def stats_update(group, carried, key_block, value_block, key_start, score_scale):

    def stats_compute(inner):
        row_max, row_sum, weighted = inner
        scores = masked_scores(group, key_block, key_start, score_scale)
        new_max = jnp.maximum(row_max, jnp.max(scores, axis=-1))
        raw_weights = jnp.exp(scores - new_max[..., None])
        grad_probs = jnp.einsum(
            "lrkgd,nkd->lkgrn", group[1], value_block, preferred_element_type=jnp.float32
        )
        rescale = jnp.exp(row_max - new_max)
        return (
            new_max,
            row_sum * rescale + jnp.sum(raw_weights, axis=-1),
            weighted * rescale + jnp.sum(raw_weights * grad_probs, axis=-1),
        )

    return lax.cond(key_start > jnp.max(group[3]), lambda inner: inner, stats_compute, carried)


def grads_update(group, row_stats, carried, key_block, value_block, key_start, score_scale):
    log_norm, row_delta = row_stats

    def grads_compute(inner):
        query_acc, key_buffer, value_buffer = inner
        scores = masked_scores(group, key_block, key_start, score_scale)
        prob_rows = jnp.exp(scores - log_norm[..., None])
        grad_probs = jnp.einsum(
            "lrkgd,nkd->lkgrn", group[1], value_block, preferred_element_type=jnp.float32
        )
        grad_scores = prob_rows * (grad_probs - row_delta[..., None])
        grad_low = grad_scores.astype(jnp.bfloat16)
        prob_low = prob_rows.astype(jnp.bfloat16)
        query_acc = query_acc + jnp.einsum(
            "lkgrn,nkd->lrkgd", grad_low, key_block, preferred_element_type=jnp.float32
        )
        key_part = jnp.einsum(
            "lkgrn,lrkgd->nkd", grad_low, group[0], preferred_element_type=jnp.float32
        )
        value_part = jnp.einsum(
            "lkgrn,lrkgd->nkd", prob_low, group[1], preferred_element_type=jnp.float32
        )
        block_rows = key_block.shape[0]
        key_buffer = lax.dynamic_update_slice_in_dim(
            key_buffer,
            lax.dynamic_slice_in_dim(key_buffer, key_start, block_rows, 0) + key_part,
            key_start,
            0,
        )
        value_buffer = lax.dynamic_update_slice_in_dim(
            value_buffer,
            lax.dynamic_slice_in_dim(value_buffer, key_start, block_rows, 0) + value_part,
            key_start,
            0,
        )
        return (query_acc, key_buffer, value_buffer)

    return lax.cond(key_start > jnp.max(group[3]), lambda inner: inner, grads_compute, carried)


def layer_pass(groups, keys, values, score_scale, total_rows):
    stat_init = []
    for group in groups:
        layer_count, row_count, key_heads, group_size, head_width = group[0].shape
        stat_shape = (layer_count, key_heads, group_size, row_count)
        stat_init.append(
            (
                jnp.full(stat_shape, NEG_START, jnp.float32),
                jnp.zeros(stat_shape, jnp.float32),
                jnp.zeros(stat_shape, jnp.float32),
            )
        )

    def advance(inner, sliced, key_start):
        return tuple(
            (
                stats_update(group, member, sliced[0], sliced[1], key_start, score_scale)
                for group, member in zip(groups, inner)
            )
        )

    gathered_stats = over_blocks(
        advance,
        tuple(stat_init),
        (
            lax.all_gather(keys, "seq", axis=0, tiled=True),
            lax.all_gather(values, "seq", axis=0, tiled=True),
        ),
    )
    row_stats = tuple(
        ((member[0] + jnp.log(member[1]), member[2] / member[1]) for member in gathered_stats)
    )
    buffer_shape = (total_rows, keys.shape[1], keys.shape[2])
    grad_init = (
        tuple((jnp.zeros(group[0].shape, jnp.float32) for group in groups)),
        jnp.zeros(buffer_shape, jnp.float32),
        jnp.zeros(buffer_shape, jnp.float32),
    )

    def advance(inner, sliced, key_start):
        query_accs, key_buffer, value_buffer = inner
        updated = []
        for group, stats_pair, query_acc in zip(groups, row_stats, query_accs):
            query_acc, key_buffer, value_buffer = grads_update(
                group,
                stats_pair,
                (query_acc, key_buffer, value_buffer),
                sliced[0],
                sliced[1],
                key_start,
                score_scale,
            )
            updated.append(query_acc)
        return (tuple(updated), key_buffer, value_buffer)

    query_accs, key_buffer, value_buffer = over_blocks(
        advance,
        grad_init,
        (
            lax.all_gather(keys, "seq", axis=0, tiled=True),
            lax.all_gather(values, "seq", axis=0, tiled=True),
        ),
    )
    key_own, value_own = (
        lax.psum_scatter(key_buffer, "seq", scatter_dimension=0, tiled=True),
        lax.psum_scatter(value_buffer, "seq", scatter_dimension=0, tiled=True),
    )
    return (query_accs, key_own, value_own)


def per_device(queries, grad_out, keys, values, doc_start):
    layer_count = queries.shape[0]
    head_width = queries.shape[3]
    key_heads = keys.shape[1]
    score_scale = 1.0 / math.sqrt(head_width)
    regrouped, regrads = (
        lax.all_to_all(queries, "head", split_axis=2, concat_axis=1, tiled=True),
        lax.all_to_all(grad_out, "head", split_axis=2, concat_axis=1, tiled=True),
    )
    row_count = regrouped.shape[1]
    local_heads = regrouped.shape[2]
    group_size = local_heads // key_heads
    five_shape = (layer_count, row_count, key_heads, group_size, head_width)
    query_rows = regrouped.reshape(five_shape)
    grad_rows = regrads.reshape(five_shape)
    seq_index = lax.axis_index("seq")
    seq_count = lax.axis_size("seq")
    total_rows = row_count * seq_count
    offsets = jnp.arange(row_count, dtype=jnp.int32)
    own_pos = seq_index * row_count + offsets
    own_start = lax.dynamic_slice_in_dim(doc_start, seq_index * row_count, row_count, 0)
    groups = ((query_rows, grad_rows, own_start, own_pos),)
    collected = []
    for layer_index in range(layer_count):
        sliced = tuple(
            (
                (
                    group[0][layer_index : layer_index + 1],
                    group[1][layer_index : layer_index + 1],
                    group[2],
                    group[3],
                )
                for group in groups
            )
        )
        accs, key_own, value_own = layer_pass(sliced, keys, values, score_scale, total_rows)
        collected.append(accs)
        if layer_index == 0:
            key_total, value_total = (key_own, value_own)
        else:
            key_total, value_total = (key_total + key_own, value_total + value_own)
    query_accs = tuple(
        (
            jnp.concatenate([accs[member] for accs in collected], axis=0)
            for member in range(len(groups))
        )
    )
    query_low = tuple(((acc * score_scale).astype(jnp.bfloat16) for acc in query_accs))
    query_final = query_low[0]
    query_final = query_final.reshape(layer_count, row_count, local_heads, head_width)
    query_grads = lax.all_to_all(query_final, "head", split_axis=1, concat_axis=2, tiled=True)
    key_grads = (key_total * score_scale).astype(jnp.bfloat16)
    value_grads = value_total.astype(jnp.bfloat16)
    return (query_grads, key_grads, value_grads)


def solution(mesh):
    in_specs = (
        P(None, ("seq", "head"), None, None),
        P(None, ("seq", "head"), None, None),
        P("seq", "head", None),
        P("seq", "head", None),
        P(),
    )
    out_specs = (
        P(None, ("seq", "head"), None, None),
        P("seq", "head", None),
        P("seq", "head", None),
    )
    return jax.shard_map(
        per_device, mesh=mesh, in_specs=in_specs, out_specs=out_specs, check_vma=False
    )
```

profile of v0, /device:TPU:0, one launch (start us, length us, event | category | flops | bytes accessed | tf_op | source)
XLA Modules:
  0.0 597.9 jit_solution(12327094851569278671)
XLA Ops:
  7.2 0.0 all-gather.3.cloned.1.call-start
  7.2 0.7 all-gather.3.cloned.1.call-update
  7.9 0.0 all-gather.5.cloned.1.call-start
  7.9 0.7 all-gather.5.cloned.1.call-update
  8.6 2.0 copy.50
  10.6 5.4 all-to-all-start
  16.0 2.0 copy.52
  18.0 8.9 %all-to-all-done = bf16[2,64,20,128]{3,1,0,2:T(8,128)(2,1)S(1)} async-done(((bf16[2,64,20,128]{3,1,0,2:T(8,128)(2,1)}), bf16[2,64,20,128]{3,1,0,2:T(8,128)(2,1)S(1)}, u32[]{:S(2)}, u32[]{:S(2)}) %all-to-all-start) | async-done | bytes 655392 | tf_op jit(solution)/shard_map/all_to_all | solution.py:178
  26.9 3.5 all-to-all-start.1
  30.4 0.0 reduce-scatter.5.cloned.1.call-start
  30.5 0.6 add_reduce_fusion
  31.1 0.8 dynamic_slice.139
  31.9 8.5 %all-to-all-done.1 = bf16[2,64,20,128]{3,1,0,2:T(8,128)(2,1)S(1)} async-done(((bf16[2,64,20,128]{3,1,0,2:T(8,128)(2,1)}), bf16[2,64,20,128]{3,1,0,2:T(8,128)(2,1)S(1)}, u32[]{:S(2)}, u32[]{:S(2)}) %all-to-all-start.1) | async-done | bytes 655392 | tf_op jit(solution)/shard_map/all_to_all | solution.py:179
  40.5 15.7 %all-gather.3.cloned.1.call-done = bf16[8192,1,128]{2,0,1:T(8,128)(2,1)} async-done(((bf16[256,1,128]{2,0,1:T(8,128)(2,1)}), bf16[8192,1,128]{2,0,1:T(8,128)(2,1)}) %all-gather.3.cloned.1.call-update) | async-done | bytes 2097168 | tf_op jit(solution)/shard_map/all_gather | solution.py:161
  56.2 45.1 %all-gather.5.cloned.1.call-done = bf16[8192,1,128]{2,0,1:T(8,128)(2,1)} async-done(((bf16[256,1,128]{2,0,1:T(8,128)(2,1)}), bf16[8192,1,128]{2,0,1:T(8,128)(2,1)}) %all-gather.5.cloned.1.call-update) | async-done | bytes 2097168 | tf_op jit(solution)/shard_map/all_gather | solution.py:162
  101.3 10.8 %while.76 = (s32[]{:T(128)}, f32[1,1,5,256]{3,2,1,0:T(8,128)S(1)}, f32[1,1,5,256]{3,2,1,0:T(8,128)S(1)}, f32[1,1,5,256]{3,2,1,0:T(8,128)S(1)}, s32[]{:T(128)}, /...) while((s32[]{:T(128)}, f32[1,1,5,256]{3,2,1,0:T(8,128)S(1)}, ...), condition=%wide.region_7.8_spmd.clone, body=%wide.region_1.7_spmd.clone.sunk | while | flops 687608832 | bytes 18062672 | solution.py:28
  101.9 5.9 conditional.12
  101.9 0.3 compare_and_fusion
  102.2 1.9 fusion.10
  104.1 2.5 fusion.8
  106.6 1.1 fusion.9
  112.2 10.8 %while.78 = (s32[]{:T(128)}, f32[1,1,5,256]{3,2,1,0:T(8,128)S(1)}, f32[1,1,5,256]{3,2,1,0:T(8,128)S(1)}, f32[1,1,5,256]{3,2,1,0:T(8,128)S(1)}, s32[]{:T(128)}, /...) while((s32[]{:T(128)}, f32[1,1,5,256]{3,2,1,0:T(8,128)S(1)}, ...), condition=%wide.region_18.19_spmd.clone, body=%wide.region_12.18_spmd.clone.sunk | while | flops 687608832 | bytes 18062672 | solution.py:28
  112.7 5.9 conditional.14
  112.8 0.3 compare_and_fusion.2
  113.1 1.9 fusion.60
  115.0 2.5 fusion.58
  117.5 1.1 fusion.59
  123.1 2.2 broadcast.98.clone.1
  125.3 2.2 broadcast.98.clone
  127.5 16.9 %while.79 = (s32[]{:T(128)}, f32[1,256,1,5,128]{1,4,3,0,2:T(8,128)S(1)}, f32[8192,1,128]{2,0,1:T(8,128)}, f32[8192,1,128]{2,0,1:T(8,128)}, s32[]{:T(128)}, /*ind...) while((s32[]{:T(128)}, ...), condition=%wide.region_22.23_spmd.clone, body=%wide.region_19.22_spmd.clone.sunk | while | flops 1692042496 | bytes 29913476 | solution.py:28
  128.1 12.2 %conditional.15 = ((f32[1,256,1,5,128]{1,4,3,0,2:T(8,128)S(1)}, f32[8192,1,128]{2,0,1:T(8,128)}, f32[8192,1,128]{2,0,1:T(8,128)})) conditional(s32[]{:T(128)} %convert_element_type.110, (s32[]{:T(128)}, bf16[8192,1,128]{2,0,1:T(8,128)(2,1)}, s32[256]{0:T(256)S(1)}, s32[]{:T(128)}, bf16[1,256,1,5,128]{4,1,3,2,0:T(8,128)(2,1)S(1)}, ...), branch_computations={%region_20.0_spmd, %region_21.21_spmd} | conditional | flops 1692042496 | bytes 29912158 | solution.py:99
  128.1 0.3 compare_and_fusion.3
  128.4 1.8 fusion.95
  130.2 2.6 fusion.76
  132.8 3.2 fusion.89
  135.9 1.5 fusion.85
  137.5 2.7 fusion.84
  144.5 2.2 broadcast.98.clone.2
  146.7 2.2 broadcast.98.clone.3
  149.0 16.9 %while.77 = (s32[]{:T(128)}, f32[1,256,1,5,128]{1,4,3,0,2:T(8,128)S(1)}, f32[8192,1,128]{2,0,1:T(8,128)}, f32[8192,1,128]{2,0,1:T(8,128)}, s32[]{:T(128)}, /*ind...) while((s32[]{:T(128)}, ...), condition=%wide.region_11.0_spmd.clone, body=%wide.region_8.11_spmd.clone.sunk | while | flops 1692042496 | bytes 29913476 | solution.py:28
  149.5 12.2 %conditional.13 = ((f32[1,256,1,5,128]{1,4,3,0,2:T(8,128)S(1)}, f32[8192,1,128]{2,0,1:T(8,128)}, f32[8192,1,128]{2,0,1:T(8,128)})) conditional(s32[]{:T(128)} %convert_element_type.108, (s32[]{:T(128)}, bf16[8192,1,128]{2,0,1:T(8,128)(2,1)}, s32[256]{0:T(256)S(1)}, s32[]{:T(128)}, bf16[1,256,1,5,128]{4,1,3,2,0:T(8,128)(2,1)S(1)}, ...), branch_computations={%region_9.9_spmd, %region_10.10_spmd} | conditional | flops 1692042496 | bytes 29912158 | solution.py:99
  149.6 0.3 compare_and_fusion.1
  149.9 1.8 fusion.45
  151.7 2.6 fusion.26
  154.3 3.2 fusion.39
  157.5 1.6 fusion.35
  159.0 2.7 fusion.34
  165.9 5.8 add.283
  171.8 0.0 reduce-scatter.5.cloned.1.call-update
  171.8 0.3 reduce-scatter.3.cloned.1.call-start
  172.1 5.9 add.282
  177.9 0.0 reduce-scatter.3.cloned.1.call-update
  177.9 0.5 copy.57
  178.4 0.5 copy.54
  178.9 1.4 fusion.108
  180.3 15.5 %all_to_all.48 = bf16[2,256,5,128]{3,0,2,1:T(2,128)(2,1)S(1)} all-to-all(bf16[2,256,5,128]{3,0,2,1:T(2,128)(2,1)S(1)} %fusion.108), channel_id=1, replica_groups=mesh['seq'=32,'head'=4] {'head'}, dimensions={1} | all-to-all | bytes 1310720 | tf_op jit(solution)/shard_map/all_to_all | solution.py:222
  195.8 0.1 copy.58
  195.9 0.9 copy.59
  196.8 307.9 %reduce-scatter.5.cloned.1.call-done = f32[256,1,128]{2,0,1:T(8,128)} async-done(((f32[8192,1,128]{2,0,1:T(8,128)}), f32[256,1,128]{2,0,1:T(8,128)}) %reduce-scatter.5.cloned.1.call-update) | async-done | bytes 131088 | tf_op jit(solution)/shard_map/reduce_scatter | solution.py:167
  504.7 1.5 convert_element_type.70
  506.2 83.6 %reduce-scatter.3.cloned.1.call-done = f32[256,1,128]{2,0,1:T(8,128)} async-done(((f32[8192,1,128]{2,0,1:T(8,128)}), f32[256,1,128]{2,0,1:T(8,128)}) %reduce-scatter.3.cloned.1.call-update) | async-done | bytes 131088 | tf_op jit(solution)/shard_map/reduce_scatter | solution.py:166
  589.8 1.5 multiply_convert_fusion
  (118 shorter events, 1.3 us)
Async XLA Ops:
  7.2 49.0 %all-gather.3.cloned.1.call-start = ((), (), s32[]{:S(2)}) async-start(), calls=%async_computation.5 | async-start | bytes 2162688 | tf_op jit(solution)/shard_map/all_gather | solution.py:161
  7.9 93.4 %all-gather.5.cloned.1.call-start = ((), (), s32[]{:S(2)}) async-start(), calls=%async_computation.6 | async-start | bytes 2162688 | tf_op jit(solution)/shard_map/all_gather | solution.py:162
  10.6 16.3 %all-to-all-start = ((bf16[2,64,20,128]{3,1,0,2:T(8,128)(2,1)}), bf16[2,64,20,128]{3,1,0,2:T(8,128)(2,1)S(1)}, u32[]{:S(2)}, u32[]{:S(2)}) async-start(bf16[2,64,20,128]{3,1,0,2:T(8,128)(2,1)} %copy.50), calls=%async_computation | async-start | bytes 1310720 | tf_op jit(solution)/shard_map/all_to_all | solution.py:178
  26.9 13.5 %all-to-all-start.1 = ((bf16[2,64,20,128]{3,1,0,2:T(8,128)(2,1)}), bf16[2,64,20,128]{3,1,0,2:T(8,128)(2,1)S(1)}, u32[]{:S(2)}, u32[]{:S(2)}) async-start(bf16[2,64,20,128]{3,1,0,2:T(8,128)(2,1)} %copy.52), calls=%async_computation.1 | async-start | bytes 1310720 | tf_op jit(solution)/shard_map/all_to_all | solution.py:179
  30.4 474.3 %reduce-scatter.5.cloned.1.call-start = ((), (), s32[]{:S(2)}) async-start(), calls=%async_computation.8 | async-start | bytes 4325376 | tf_op jit(solution)/shard_map/reduce_scatter | solution.py:167
  171.8 418.0 %reduce-scatter.3.cloned.1.call-start = ((), (), s32[]{:S(2)}) async-start(), calls=%async_computation.7 | async-start | bytes 4325376 | tf_op jit(solution)/shard_map/reduce_scatter | solution.py:166
Sparse Core Ops, SparseCore 0:
  10.2 45.9 all-gather.2
  58.5 42.7 all-gather.4
  171.9 332.7 reduce-scatter.4
  508.2 81.5 reduce-scatter.2
where the time goes:
time: 603 us; the launch traced here: 598 us
  waiting for transfers between devices  471 us (78%)
  matrix products  32.5 us (5%)
  other arithmetic  20.2 us (3%)
  loops' own time  19.6 us (3%)
  local copies, waits for them, and re-layouts  16 us (3%)
  blocking collectives  15.5 us (3%)
  between operations  13.9 us (2%)
  starting transfers between devices  9.28 us (2%)
    reduce_scatter x1, waiting for transfers between devices, layer_pass(): lax.psum_scatter(value_buffer, 'seq', scatter_dimension=0, tiled=True)  308 us
    reduce_scatter x1, waiting for transfers between devices, layer_pass(): lax.psum_scatter(key_buffer, 'seq', scatter_dimension=0, tiled=True)  83.6 us
    all_gather x1, waiting for transfers between devices, layer_pass(): lax.all_gather(values, 'seq', axis=0, tiled=True)  45.1 us
    another operation x4, loops' own time, over_blocks(): return lax.fori_loop(0, key_count // block_rows, one_block, carried)  18.5 us
    all_gather x1, waiting for transfers between devices, layer_pass(): lax.all_gather(keys, 'seq', axis=0, tiled=True)  15.7 us
    all_to_all x1, blocking collectives, per_device(): lax.all_to_all(query_final, 'head', split_axis=1, concat_axis=2, tiled=True)  15.5 us
  transfers between devices with their start and end apart: 6, of which 6 were waited for; matrix products, arithmetic and copies ran while one was open for 3% of the time, Pallas kernels for 0%

commit v1 on v0

--- a/solution.py
+++ b/solution.py
@@ -159,7 +159,9 @@
         grad_init,
         (
             lax.all_gather(keys, "seq", axis=0, tiled=True),
-            lax.all_gather(values, "seq", axis=0, tiled=True),
+            jnp.concatenate(
+                lax.all_to_all(jnp.stack([values] * lax.axis_size("seq")), "seq", 0, 0), axis=0
+            ),
         ),
     )
     key_own, value_own = (

time: 603 us -> 619 us (1.027)
  blocking collectives: 15.5 us -> 27.9 us
    all_to_all x0 -> x1, blocking collectives: none -> 12.4 us  [per_device(): lax.all_to_all(grad_out, 'head', split_axis=2, concat_axis=1, tiled=True)]
    all_gather x1, waiting for transfers between devices: 45.1 us -> 57.2 us  [layer_pass(): lax.all_gather(values, 'seq', axis=0, tiled=True)]
    all_to_all x1, waiting for transfers between devices: 8.46 us -> 0.01 us  [layer_pass(): lax.all_to_all(jnp.stack([values] * lax.axis_size('seq')), 'seq', 0, 0)]
    reduce_scatter x1, waiting for transfers between devices: 308 us -> 302 us  [layer_pass(): lax.psum_scatter(value_buffer, 'seq', scatter_dimension=0, tiled=True)]
  transfers between devices with their start and end apart: 6 -> 6, of which waited for: 6 -> 5; matrix products, arithmetic and copies ran while one was open for 3% -> 5% of each run, Pallas kernels for 0% -> 0%
where the time goes in v1:
time: 619 us; the launch traced here: 615 us
  waiting for transfers between devices  466 us (75%)
  matrix products  31.5 us (5%)
  blocking collectives  27.9 us (5%)
  loops' own time  22.2 us (4%)
  other arithmetic  20.3 us (3%)
  local copies, waits for them, and re-layouts  19.8 us (3%)
  between operations  14 us (2%)
  starting transfers between devices  13.1 us (2%)
    reduce_scatter x1, waiting for transfers between devices, layer_pass(): lax.psum_scatter(value_buffer, 'seq', scatter_dimension=0, tiled=True)  302 us
    reduce_scatter x1, waiting for transfers between devices, layer_pass(): lax.psum_scatter(key_buffer, 'seq', scatter_dimension=0, tiled=True)  83.6 us
    all_gather x1, waiting for transfers between devices, layer_pass(): lax.all_gather(values, 'seq', axis=0, tiled=True)  57.2 us
    another operation x4, loops' own time, over_blocks(): return lax.fori_loop(0, key_count // block_rows, one_block, carried)  21.2 us
    all_to_all x1, blocking collectives, per_device(): lax.all_to_all(query_final, 'head', split_axis=1, concat_axis=2, tiled=True)  15.5 us
    all_gather x1, waiting for transfers between devices, layer_pass(): lax.all_gather(keys, 'seq', axis=0, tiled=True)  12.5 us
    all_to_all x1, blocking collectives, per_device(): lax.all_to_all(grad_out, 'head', split_axis=2, concat_axis=1, tiled=True)  12.4 us
  transfers between devices with their start and end apart: 6, of which 5 were waited for; matrix products, arithmetic and copies ran while one was open for 5% of the time, Pallas kernels for 0%

profile of v1, /device:TPU:0, one launch (start us, length us, event | category | flops | bytes accessed | tf_op | source)
XLA Modules:
  0.0 614.9 jit_solution(16801423045595506998)
XLA Ops:
  7.2 0.0 all-gather.3.cloned.1.call-start
  7.2 0.7 all-gather.3.cloned.1.call-update
  7.9 0.0 all-gather.5.cloned.1.call-start
  8.0 0.7 all-gather.5.cloned.1.call-update
  8.7 2.0 copy.50
  10.6 5.4 all-to-all-start
  16.1 1.1 copy.52
  17.2 9.7 %all-to-all-done = bf16[2,64,20,128]{3,1,0,2:T(8,128)(2,1)S(1)} async-done(((bf16[2,64,20,128]{3,1,0,2:T(8,128)(2,1)}), bf16[2,64,20,128]{3,1,0,2:T(8,128)(2,1)S(1)}, u32[]{:S(2)}, u32[]{:S(2)}) %all-to-all-start) | async-done | bytes 655392 | tf_op jit(solution)/shard_map/all_to_all | solution.py:180
  26.9 12.4 %all_to_all.54 = bf16[2,64,20,128]{3,1,0,2:T(8,128)(2,1)S(1)} all-to-all(bf16[2,64,20,128]{3,1,0,2:T(8,128)(2,1)S(1)} %copy.52), channel_id=1, replica_groups=mesh['seq'=32,'head'=4] {'head'}, dimensions={2} | all-to-all | bytes 1310720 | tf_op jit(solution)/shard_map/all_to_all | solution.py:181
  39.4 1.8 stack.2
  41.2 7.3 %all-to-all-start.2 = ((bf16[32,256,1,128]{3,1,2,0:T(8,128)(2,1)}), bf16[32,256,1,128]{3,1,2,0:T(8,128)(2,1)S(1)}, u32[]{:S(2)}, u32[]{:S(2)}) async-start(bf16[32,256,1,128]{3,1,2,0:T(8,128)(2,1)} %stack.2), calls=%async_computation.2 | async-start | bytes 4194304 | tf_op jit(solution)/shard_map/all_to_all | solution.py:163
  48.5 0.0 reduce-scatter.5.cloned.1.call-start
  48.6 0.7 add_reduce_fusion
  49.3 0.8 dynamic_slice.139
  50.2 0.7 copy.56
  51.0 12.5 %all-gather.3.cloned.1.call-done = bf16[8192,1,128]{2,0,1:T(8,128)(2,1)} async-done(((bf16[256,1,128]{2,0,1:T(8,128)(2,1)}), bf16[8192,1,128]{2,0,1:T(8,128)(2,1)}) %all-gather.3.cloned.1.call-update) | async-done | bytes 2097168 | tf_op jit(solution)/shard_map/all_gather | solution.py:161
  63.5 57.2 %all-gather.5.cloned.1.call-done = bf16[8192,1,128]{2,0,1:T(8,128)(2,1)} async-done(((bf16[256,1,128]{2,0,1:T(8,128)(2,1)}), bf16[8192,1,128]{2,0,1:T(8,128)(2,1)}) %all-gather.5.cloned.1.call-update) | async-done | bytes 2097168 | tf_op jit(solution)/shard_map/all_gather | solution.py:128
  120.7 11.5 %while.76 = (s32[]{:T(128)}, f32[1,1,5,256]{3,2,1,0:T(8,128)S(1)}, f32[1,1,5,256]{3,2,1,0:T(8,128)S(1)}, f32[1,1,5,256]{3,2,1,0:T(8,128)S(1)}, s32[]{:T(128)}, /...) while((s32[]{:T(128)}, f32[1,1,5,256]{3,2,1,0:T(8,128)S(1)}, ...), condition=%wide.region_7.8_spmd.clone, body=%wide.region_1.7_spmd.clone.sunk | while | flops 687608832 | bytes 18062672 | solution.py:28
  121.4 5.9 conditional.12
  121.4 0.3 compare_and_fusion
  121.7 1.9 fusion.10
  123.6 2.5 fusion.8
  126.1 1.1 fusion.9
  132.2 0.7 copy-done.1
  133.0 11.5 %while.78 = (s32[]{:T(128)}, f32[1,1,5,256]{3,2,1,0:T(8,128)S(1)}, f32[1,1,5,256]{3,2,1,0:T(8,128)S(1)}, f32[1,1,5,256]{3,2,1,0:T(8,128)S(1)}, s32[]{:T(128)}, /...) while((s32[]{:T(128)}, f32[1,1,5,256]{3,2,1,0:T(8,128)S(1)}, ...), condition=%wide.region_18.19_spmd.clone, body=%wide.region_12.18_spmd.clone.sunk | while | flops 687608832 | bytes 19373420 | solution.py:28
  133.6 5.9 conditional.14
  133.7 0.3 compare_and_fusion.2
  133.9 1.9 fusion.60
  135.9 2.5 fusion.58
  138.4 1.1 fusion.59
  144.6 2.2 broadcast.101.clone.1
  146.8 2.2 broadcast.101.clone
  149.0 16.7 %while.79 = (s32[]{:T(128)}, f32[1,256,1,5,128]{1,4,3,0,2:T(8,128)S(1)}, f32[8192,1,128]{2,0,1:T(8,128)}, f32[8192,1,128]{2,0,1:T(8,128)}, s32[]{:T(128)}, /*ind...) while((s32[]{:T(128)}, ...), condition=%wide.region_22.23_spmd.clone, body=%wide.region_19.22_spmd.clone.sunk | while | flops 1692042496 | bytes 31230368 | solution.py:28
  149.6 11.3 %conditional.15 = ((f32[1,256,1,5,128]{1,4,3,0,2:T(8,128)S(1)}, f32[8192,1,128]{2,0,1:T(8,128)}, f32[8192,1,128]{2,0,1:T(8,128)})) conditional(s32[]{:T(128)} %convert_element_type.110, (s32[]{:T(128)}, bf16[8192,1,128]{2,0,1:T(8,128)(2,1)}, s32[256]{0:T(256)S(1)}, s32[]{:T(128)}, bf16[1,256,1,5,128]{4,1,3,2,0:T(8,128)(2,1)S(1)}, ...), branch_computations={%region_20.0_spmd, %region_21.21_spmd} | conditional | flops 1692042496 | bytes 31229050 | solution.py:99
  149.7 0.3 compare_and_fusion.3
  150.0 1.8 fusion.95
  151.8 1.7 fusion.76
  153.4 3.2 fusion.89
  156.6 1.5 fusion.85
  158.2 2.7 fusion.84
  165.7 1.3 copy-done
  167.0 2.3 broadcast.101.clone.2
  169.3 2.2 broadcast.101.clone.3
  171.6 17.6 %while.77 = (s32[]{:T(128)}, f32[1,256,1,5,128]{1,4,3,0,2:T(8,128)S(1)}, f32[8192,1,128]{2,0,1:T(8,128)}, f32[8192,1,128]{2,0,1:T(8,128)}, s32[]{:T(128)}, /*ind...) while((s32[]{:T(128)}, ...), condition=%wide.region_11.0_spmd.clone, body=%wide.region_8.11_spmd.clone.sunk | while | flops 1692042496 | bytes 29913476 | solution.py:28
  172.2 12.2 %conditional.13 = ((f32[1,256,1,5,128]{1,4,3,0,2:T(8,128)S(1)}, f32[8192,1,128]{2,0,1:T(8,128)}, f32[8192,1,128]{2,0,1:T(8,128)})) conditional(s32[]{:T(128)} %convert_element_type.108, (s32[]{:T(128)}, bf16[8192,1,128]{2,0,1:T(8,128)(2,1)}, s32[256]{0:T(256)S(1)}, s32[]{:T(128)}, bf16[1,256,1,5,128]{4,1,3,2,0:T(8,128)(2,1)S(1)}, ...), branch_computations={%region_9.9_spmd, %region_10.10_spmd} | conditional | flops 1692042496 | bytes 29912158 | solution.py:99
  172.2 0.3 compare_and_fusion.1
  172.5 1.8 fusion.45
  174.3 2.6 fusion.26
  176.9 3.2 fusion.39
  180.1 1.5 fusion.35
  181.7 2.7 fusion.34
  189.1 5.8 add.283
  195.0 0.3 reduce-scatter.3.cloned.1.call-start
  195.3 5.9 add.282
  201.2 0.5 copy.57
  201.6 0.5 copy.54
  202.1 1.4 fusion.108
  203.5 15.5 %all_to_all.55 = bf16[2,256,5,128]{3,0,2,1:T(2,128)(2,1)S(1)} all-to-all(bf16[2,256,5,128]{3,0,2,1:T(2,128)(2,1)S(1)} %fusion.108), channel_id=1, replica_groups=mesh['seq'=32,'head'=4] {'head'}, dimensions={1} | all-to-all | bytes 1310720 | tf_op jit(solution)/shard_map/all_to_all | solution.py:224
  219.0 0.1 copy.58
  219.1 0.9 copy.59
  220.0 301.6 %reduce-scatter.5.cloned.1.call-done = f32[256,1,128]{2,0,1:T(8,128)} async-done(((f32[8192,1,128]{2,0,1:T(8,128)}), f32[256,1,128]{2,0,1:T(8,128)}) %reduce-scatter.5.cloned.1.call-update) | async-done | bytes 131088 | tf_op jit(solution)/shard_map/reduce_scatter | solution.py:169
  521.6 1.5 convert_element_type.70
  523.2 83.6 %reduce-scatter.3.cloned.1.call-done = f32[256,1,128]{2,0,1:T(8,128)} async-done(((f32[8192,1,128]{2,0,1:T(8,128)}), f32[256,1,128]{2,0,1:T(8,128)}) %reduce-scatter.3.cloned.1.call-update) | async-done | bytes 131088 | tf_op jit(solution)/shard_map/reduce_scatter | solution.py:168
  606.8 1.5 multiply_convert_fusion
  (130 shorter events, 1.3 us)
Async XLA Ops:
  7.2 32.2 %copy-start.5 = (bf16[256,1,128]{2,0,1:T(8,128)(2,1)S(1)}, bf16[256,1,128]{2,0,1:T(8,128)(2,1)}, u32[]{:S(2)}) copy-start(bf16[256,1,128]{2,0,1:T(8,128)(2,1)} %param.24) | copy-start | bytes 196612
  7.2 56.3 %all-gather.3.cloned.1.call-start = ((), (), s32[]{:S(2)}) async-start(), calls=%async_computation.6 | async-start | bytes 2162688 | tf_op jit(solution)/shard_map/all_gather | solution.py:161
  7.9 112.8 %all-gather.5.cloned.1.call-start = ((), (), s32[]{:S(2)}) async-start(), calls=%async_computation.7 | async-start | bytes 2162688 | tf_op jit(solution)/shard_map/all_gather | solution.py:128
  10.6 16.3 %all-to-all-start = ((bf16[2,64,20,128]{3,1,0,2:T(8,128)(2,1)}), bf16[2,64,20,128]{3,1,0,2:T(8,128)(2,1)S(1)}, u32[]{:S(2)}, u32[]{:S(2)}) async-start(bf16[2,64,20,128]{3,1,0,2:T(8,128)(2,1)} %copy.50), calls=%async_computation | async-start | bytes 1310720 | tf_op jit(solution)/shard_map/all_to_all | solution.py:180
  41.2 103.3 %all-to-all-start.2 = ((bf16[32,256,1,128]{3,1,2,0:T(8,128)(2,1)}), bf16[32,256,1,128]{3,1,2,0:T(8,128)(2,1)S(1)}, u32[]{:S(2)}, u32[]{:S(2)}) async-start(bf16[32,256,1,128]{3,1,2,0:T(8,128)(2,1)} %stack.2), calls=%async_computation.2 | async-start | bytes 4194304 | tf_op jit(solution)/shard_map/all_to_all | solution.py:163
  48.5 473.1 %reduce-scatter.5.cloned.1.call-start = ((), (), s32[]{:S(2)}) async-start(), calls=%async_computation.9 | async-start | bytes 4325376 | tf_op jit(solution)/shard_map/reduce_scatter | solution.py:169
  132.2 0.7 copy-start.1
  133.6 2.2 copy-start.3
  149.6 2.1 copy-start.4
  165.7 1.3 copy-start
  167.0 4.6 copy-start.2
  195.0 411.8 %reduce-scatter.3.cloned.1.call-start = ((), (), s32[]{:S(2)}) async-start(), calls=%async_computation.8 | async-start | bytes 4325376 | tf_op jit(solution)/shard_map/reduce_scatter | solution.py:168
Sparse Core Ops, SparseCore 0:
  10.2 53.2 all-gather.2
  65.8 54.9 all-gather.4
  195.1 326.4 reduce-scatter.4
  525.1 81.6 reduce-scatter.2
